TPU v7x, 32 devices: a whole 2x2x4 slice. The times are simulated.
32 devices in a mesh: dp: 8 (over y, x, core), mp: 4 (over z).
Axes of the slice: x: 2, y: 2, z: 4, core: 2. Of those that a mesh axis runs over, the one named last changes fastest.
Arguments:
- tokens: bfloat16 [2, 1024, 4096], P(None, 'dp', 'mp'), may hold values from -6 to 6
- targets: bfloat16 [2, 1024, 4096], P(None, 'dp', 'mp'), may hold values from -6 to 6
- weight: bfloat16 [4096, 4096], P('mp'), may hold values from -0.09375 to 0.09375
- basis: bfloat16 [4096, 512], replicated, may hold values from -0.09375 to 0.09375
- moment1: float32 [4, 1024, 512], P('mp', 'dp'), may hold values from -0.06 to 0.06
- moment2: float32 [4, 1024, 512], P('mp', 'dp'), may hold values from 1e-05 to 0.001
Outputs:
- new_weight: bfloat16 [4096, 4096], P('mp')
- new_moment1: float32 [4, 1024, 512], P('mp', 'dp')
- new_moment2: float32 [4, 1024, 512], P('mp', 'dp')
All inputs are finite; a program needn't handle non-finite values.
Results may differ from a plain program's by a relative error of at most 0.009.
Values may be sent and summed in bfloat16 or wider, within the bound.
A program may use at most 64 MiB of HBM per device.

v0:
```python
import jax
import jax.numpy as jnp
from jax import lax
from jax.sharding import PartitionSpec as P


def local(tokens, targets, weight, basis, moment1, moment2):
    whole = lax.all_gather(tokens, "mp", axis=2, tiled=True)
    total_tokens = tokens.shape[1] * lax.axis_size("dp")
    owned_rows = moment1.shape[1]
    first = moment1[0]
    second = moment2[0]
    current = weight
    for turn in range(2):
        inputs = whole[turn]
        outputs = lax.dot_general(
            inputs, current, (((1,), (1,)), ((), ())), preferred_element_type=jnp.float32
        ).astype(jnp.bfloat16)
        errors = (outputs.astype(jnp.float32) - targets[turn].astype(jnp.float32)).astype(
            jnp.bfloat16
        )
        reduced = jnp.dot(inputs, basis, preferred_element_type=jnp.float32)
        part_errors = errors.astype(jnp.float32)
        projected = (
            lax.psum_scatter(
                lax.dot_general(
                    part_errors, reduced, (((0,), (0,)), ((), ())), precision=lax.Precision.HIGHEST
                ),
                "dp",
                scatter_dimension=0,
                tiled=True,
            )
            / total_tokens
        )
        first = 0.9 * first + 0.1 * projected
        second = 0.95 * second + 0.05 * projected * projected
        direction = (first / (jnp.sqrt(second) + 1e-08)).astype(jnp.bfloat16)
        own_weight = lax.dynamic_slice_in_dim(
            current, lax.axis_index("dp") * owned_rows, owned_rows, 0
        )
        lifted = lax.dot_general(
            direction, basis, (((1,), (1,)), ((), ())), preferred_element_type=jnp.float32
        )
        new_rows = (own_weight.astype(jnp.float32) - 0.02 * lifted).astype(jnp.bfloat16)
        current = lax.all_gather(new_rows, "dp", axis=0, tiled=True)
    return (current, first[None], second[None])


def solution(mesh):
    in_specs = (
        P(None, "dp", "mp"),
        P(None, "dp", "mp"),
        P("mp", None),
        P(),
        P("mp", "dp", None),
        P("mp", "dp", None),
    )
    out_specs = (P("mp", None), P("mp", "dp", None), P("mp", "dp", None))
    return jax.shard_map(local, mesh=mesh, in_specs=in_specs, out_specs=out_specs, check_vma=False)
```

profile of v0, /device:TPU:0, one launch (start us, length us, event | category | flops | bytes accessed | tf_op | source)
XLA Modules:
  0.0 293.4 jit_solution(11323379693087445901)
XLA Ops:
  7.2 0.0 copy-start.5
  7.2 0.0 all-gather.4.cloned.1.call-start
  7.2 0.7 all-gather.4.cloned.1.call-update
  7.9 0.0 reduce-scatter.3.cloned.1.call-start
  8.0 50.0 %all-gather.4.cloned.1.call-done = bf16[2,128,4096]{2,1,0:T(8,128)(2,1)} async-done(((bf16[2,128,1024]{2,1,0:T(8,128)(2,1)}), bf16[2,128,4096]{2,1,0:T(8,128)(2,1)}) %all-gather.4.cloned.1.call-update) | async-done | bytes 2097168 | tf_op jit(solution)/shard_map/all_gather | solution.py:8
  58.0 0.0 copy-start
  58.0 3.4 %fusion.11 = f32[128,512]{1,0:T(8,128)S(1)} fusion(bf16[4096,512]{1,0:T(8,128)(2,1)} %param.9, bf16[2,128,4096]{2,1,0:T(8,128)(2,1)} %all-gather.4.cloned.1.call-done), kind=kOutput, calls=%fused_computation.17 | convolution fusion | flops 536870912 | bytes 5505024 | tf_op jit(solution)/shard_map/dot_general | solution.py:22
  61.3 0.0 copy-done.5
  61.4 0.0 copy-done
  61.4 6.3 %fusion.10 = bf16[128,1024]{1,0:T(8,128)(2,1)S(1)} fusion(bf16[1024,4096]{1,0:T(8,128)(2,1)} %param.8, bf16[2,128,4096]{2,1,0:T(8,128)(2,1)S(1)} %copy-done, bf16[2,128,1024]{2,1,0:T(8,128)(2,1)S(1)} %copy-done.5), kind=kOutput, calls=%fused_computation.14 | convolution fusion | flops 1074397184 | bytes 9961472 | tf_op jit(solution)/shard_map/dot_general | solution.py:16
  67.6 0.0 copy-start.1
  67.6 0.0 copy-start.2
  67.7 2.4 fusion.24
  70.0 0.0 reduce-scatter.3.cloned.1.call-update
  70.0 0.0 all-gather.6.cloned.1.call-start
  70.1 40.0 %reduce-scatter.3.cloned.1.call-done = f32[128,512]{1,0:T(8,128)} async-done(((f32[1024,512]{1,0:T(8,128)}), f32[128,512]{1,0:T(8,128)}) %reduce-scatter.3.cloned.1.call-update) | async-done | bytes 262160 | tf_op jit(solution)/shard_map/reduce_scatter | solution.py:25
  110.1 0.0 copy-done.1
  110.1 0.0 copy-done.2
  110.1 5.0 %fusion.2 = bf16[128,4096]{1,0:T(8,128)(2,1)} fusion(bf16[4096,512]{1,0:T(8,128)(2,1)} %param.9, bf16[1024,4096]{1,0:T(8,128)(2,1)} %param.8, s32[]{:T(128)S(6)} %select_n.4, f32[128,512]{1,0:T(8,128)} %reduce-scatter.3.cloned.1.call-done, f32[1,128,512]{2,1,0:T(8,128)S(1)} %copy-done.1, f32[1,128,512]{2,1,0:T(8,128)S(1)} %copy-done.2), kind=kOutput, calls=%fused_computation.4 | convolution fusion | flops 539688960 | bytes 7077892 | tf_op jit(solution)/shard_map/dot_general | solution.py:41
  115.1 0.0 all-gather.6.cloned.1.call-update
  115.1 0.0 reduce-scatter.5.cloned.1.call-start
  115.2 2.9 fusion.12
  118.1 51.5 %all-gather.6.cloned.1.call-done = bf16[1024,4096]{1,0:T(8,128)(2,1)} async-done(((bf16[128,4096]{1,0:T(8,128)(2,1)}), bf16[1024,4096]{1,0:T(8,128)(2,1)}) %all-gather.6.cloned.1.call-update) | async-done | bytes 8388624 | tf_op jit(solution)/shard_map/all_gather | solution.py:45
  169.5 6.3 %fusion.7 = bf16[128,1024]{1,0:T(8,128)(2,1)S(1)} fusion(bf16[1024,4096]{1,0:T(8,128)(2,1)} %all-gather.6.cloned.1.call-done, bf16[2,128,4096]{2,1,0:T(8,128)(2,1)S(1)} %copy-done, bf16[2,128,1024]{2,1,0:T(8,128)(2,1)S(1)} %copy-done.5), kind=kOutput, calls=%fused_computation.10 | convolution fusion | flops 1074397184 | bytes 9961472 | tf_op jit(solution)/shard_map/dot_general | solution.py:16
  175.8 0.0 copy-start.3
  175.8 2.4 fusion.25
  178.2 0.0 reduce-scatter.5.cloned.1.call-update
  178.2 0.0 all-gather.8.cloned.1.call-start
  178.2 41.2 %reduce-scatter.5.cloned.1.call-done = f32[128,512]{1,0:T(8,128)} async-done(((f32[1024,512]{1,0:T(8,128)}), f32[128,512]{1,0:T(8,128)}) %reduce-scatter.5.cloned.1.call-update) | async-done | bytes 262160 | tf_op jit(solution)/shard_map/reduce_scatter | solution.py:25
  219.4 0.0 copy-done.3
  219.4 0.0 copy-start.4
  219.4 5.1 %fusion.3 = bf16[128,4096]{1,0:T(8,128)(2,1)} fusion(bf16[4096,512]{1,0:T(8,128)(2,1)} %param.9, bf16[1024,4096]{1,0:T(8,128)(2,1)} %all-gather.6.cloned.1.call-done, s32[]{:T(128)S(6)} %select_n.4, f32[128,512]{1,0:T(8,128)} %reduce-scatter.5.cloned.1.call-done, f32[128,512]{1,0:T(8,128)S(1)} %copy-done.3, f32[1,128,512]{2,1,0:T(8,128)S(1)} %copy-done.1, ...), kind=kOutput, calls=%fused_computation.5 | convolution fusion | flops 540213248 | bytes 7340036 | tf_op jit(solution)/shard_map/dot_general | solution.py:41
  224.5 0.0 all-gather.8.cloned.1.call-update
  224.6 0.0 copy-done.4
  224.6 0.9 fusion.16
  225.5 53.5 %all-gather.8.cloned.1.call-done = bf16[1024,4096]{1,0:T(8,128)(2,1)} async-done(((bf16[128,4096]{1,0:T(8,128)(2,1)}), bf16[1024,4096]{1,0:T(8,128)(2,1)}) %all-gather.8.cloned.1.call-update) | async-done | bytes 8388624 | tf_op jit(solution)/shard_map/all_gather | solution.py:45
  279.0 7.9 %copy.10 = bf16[1024,4096]{1,0:T(8,128)(2,1)} copy(bf16[1024,4096]{1,0:T(8,128)(2,1)} %all-gather.8.cloned.1.call-done) | data formatting | bytes 16777216
Async XLA Ops:
  7.2 54.2 %copy-start.5 = (bf16[2,128,1024]{2,1,0:T(8,128)(2,1)S(1)}, bf16[2,128,1024]{2,1,0:T(8,128)(2,1)}, u32[]{:S(2)}) copy-start(bf16[2,128,1024]{2,1,0:T(8,128)(2,1)} %param.7) | copy-start | bytes 1572868
  7.2 50.8 %all-gather.4.cloned.1.call-start = ((), (), s32[]{:S(2)}) async-start(), calls=%async_computation.2 | async-start | bytes 2621440 | tf_op jit(solution)/shard_map/all_gather | solution.py:8
  7.9 102.2 %reduce-scatter.3.cloned.1.call-start = ((), (), s32[]{:S(2)}) async-start(), calls=%async_computation.3 | async-start | bytes 2359296 | tf_op jit(solution)/shard_map/reduce_scatter | solution.py:25
  58.0 3.4 %copy-start = (bf16[2,128,4096]{2,1,0:T(8,128)(2,1)S(1)}, bf16[2,128,4096]{2,1,0:T(8,128)(2,1)}, u32[]{:S(2)}) copy-start(bf16[2,128,4096]{2,1,0:T(8,128)(2,1)} %all-gather.4.cloned.1.call-done) | copy-start | bytes 6291460
  67.6 42.5 %copy-start.1 = (f32[1,128,512]{2,1,0:T(8,128)S(1)}, f32[1,128,512]{2,1,0:T(8,128)}, u32[]{:S(2)}) copy-start(f32[1,128,512]{2,1,0:T(8,128)} %param.10) | copy-start | bytes 786436
  67.6 42.5 %copy-start.2 = (f32[1,128,512]{2,1,0:T(8,128)S(1)}, f32[1,128,512]{2,1,0:T(8,128)}, u32[]{:S(2)}) copy-start(f32[1,128,512]{2,1,0:T(8,128)} %param.11) | copy-start | bytes 786436
  70.0 99.5 %all-gather.6.cloned.1.call-start = ((), (), s32[]{:S(2)}) async-start(), calls=%async_computation.4 | async-start | bytes 9437184 | tf_op jit(solution)/shard_map/all_gather | solution.py:45
  115.1 104.3 %reduce-scatter.5.cloned.1.call-start = ((), (), s32[]{:S(2)}) async-start(), calls=%async_computation.5 | async-start | bytes 2359296 | tf_op jit(solution)/shard_map/reduce_scatter | solution.py:25
  175.8 43.6 %copy-start.3 = (f32[128,512]{1,0:T(8,128)S(1)}, f32[128,512]{1,0:T(8,128)}, u32[]{:S(2)}) copy-start(f32[128,512]{1,0:T(8,128)} %reduce-scatter.3.cloned.1.call-done) | copy-start | bytes 786436
  178.2 100.8 %all-gather.8.cloned.1.call-start = ((), (), s32[]{:S(2)}) async-start(), calls=%async_computation.6 | async-start | bytes 9437184 | tf_op jit(solution)/shard_map/all_gather | solution.py:45
  219.4 5.1 %copy-start.4 = (f32[128,512]{1,0:T(8,128)S(1)}, f32[128,512]{1,0:T(8,128)}, u32[]{:S(2)}) copy-start(f32[128,512]{1,0:T(8,128)} %reduce-scatter.5.cloned.1.call-done) | copy-start | bytes 786436
Sparse Core Ops, SparseCore 0:
  9.6 48.3 all-gather.3
  70.2 39.9 reduce-scatter.2
  115.2 54.2 all-gather.5
  178.3 41.0 reduce-scatter.4
  224.7 54.2 all-gather.7
where the time goes:
time: 294 us; the launch traced here: 293 us
  waiting for transfers between devices  237 us (81%)
  matrix products  33.6 us (11%)
  between operations  13.9 us (5%)
  local copies, waits for them, and re-layouts  7.91 us (3%)
    all_gather x2, waiting for transfers between devices, local(): current = lax.all_gather(new_rows, 'dp', axis=0, tiled=True)  105 us
    reduce_scatter x2, waiting for transfers between devices, local(): lax.psum_scatter(lax.dot_general(part_errors, reduced, (((0,), (0,)), (()...  81.2 us
    all_gather x1, waiting for transfers between devices, local(): whole = lax.all_gather(tokens, 'mp', axis=2, tiled=True)  50 us
    dot_general x2, matrix products, local(): lax.dot_general(inputs, current, (((1,), (1,)), ((), ())), preferred_elem...  12.5 us
    dot_general x2, matrix products, local(): lax.dot_general(direction, basis, (((1,), (1,)), ((), ())), preferred_ele...  10.1 us
    unnamed x13, local copies, waits for them, and re-layouts  7.91 us
    dot_general x2, matrix products, local(): reduced = jnp.dot(inputs, basis, preferred_element_type=jnp.float32)  6.28 us
  transfers between devices with their start and end apart: 5, of which 5 were waited for; matrix products, arithmetic and copies ran while one was open for 1% of the time, Pallas kernels for 0%

commit v1 on v0

v1 whole, which is shorter than its diff:
```python
import functools

import jax
import jax.numpy as jnp
from jax import lax
from jax.experimental import pallas as pl
from jax.experimental.pallas import tpu as pltpu
from jax.sharding import PartitionSpec as P

F32 = jnp.float32
BF16 = jnp.bfloat16


def dot_nt(a, b):
    return lax.dot_general(a, b, (((1,), (1,)), ((), ())), preferred_element_type=F32)


def dot_tn(a, b):
    return lax.dot_general(a, b, (((0,), (0,)), ((), ())), preferred_element_type=F32)


def kernel(
    n_dp, n_mp, total_tokens,
    tok, tgt_hbm, w_hbm, b_hbm, m_hbm, v_hbm,
    w1_hbm, d1_hbm, m_out, v_out,
    xbuf, tgt, w, b, mom1, mom2, y, r, e, g, send1, recv1, send2, recv2, dall,
    l_sem, x_send, x_recv, s1_send, s1_recv, s2_send, s2_recv, d_send, d_recv, o_sem,
):
    dp = lax.axis_index("dp")
    mp = lax.axis_index("mp")
    core = lax.rem(dp, 2)
    chip = lax.div(dp, 2)
    partner = dp + 1 - 2 * core
    n_ch = n_dp // 2
    out_rows, features = w_hbm.shape
    rows = out_rows // n_dp
    fin = features // n_mp
    rank = b_hbm.shape[1]
    tile = min(256, out_rows)
    tiles = out_rows // tile

    def mp_at(k):
        return lax.rem(mp + k, n_mp)

    def chip_at(k):
        return lax.rem(chip + k, n_ch)

    def columns(j):
        return pl.ds(pl.multiple_of(j * fin, fin), fin)

    def owner_rows(i):
        return pl.ds(pl.multiple_of(i * rows, rows), rows)

    def tile_at(i):
        return pl.ds(pl.multiple_of(i * tile, tile), tile)

    def remote(src, dst, send, recv, where):
        return pltpu.make_async_remote_copy(
            src_ref=src, dst_ref=dst, send_sem=send, recv_sem=recv,
            device_id=where, device_id_type=pl.DeviceIdType.MESH,
        )

    w_copies = []
    for k in range(n_mp):
        j = mp_at(k)
        w_copies.append(pltpu.make_async_copy(w_hbm.at[:, columns(j)], w.at[j], l_sem.at[k]))
    b_copy = pltpu.make_async_copy(b_hbm, b, l_sem.at[n_mp])
    t_copy = pltpu.make_async_copy(tgt_hbm, tgt, l_sem.at[n_mp + 1])
    m_copy = pltpu.make_async_copy(m_hbm.at[0], mom1, l_sem.at[n_mp + 2])
    v_copy = pltpu.make_async_copy(v_hbm.at[0], mom2, l_sem.at[n_mp + 3])
    b_copy.start()
    for copy in w_copies:
        copy.start()
    t_copy.start()
    m_copy.start()
    v_copy.start()

    barrier = pltpu.get_barrier_semaphore()
    peers = [(dp, mp_at(k)) for k in range(1, n_mp)]
    peers += [(chip_at(k) * 2 + core, mp) for k in range(1, n_ch)]
    peers += [(partner, mp)]
    for peer in peers:
        pl.semaphore_signal(barrier, inc=1, device_id=peer, device_id_type=pl.DeviceIdType.MESH)
    pl.semaphore_wait(barrier, len(peers))

    sends = []
    for s in range(2):
        for k in range(1, n_mp):
            copy = remote(
                tok.at[s], xbuf.at[s, mp], x_send.at[s, k], x_recv.at[s, mp], (dp, mp_at(k))
            )
            copy.start()
            sends.append(copy)

    def block(s, j, x, first):
        @pl.loop(0, tiles)
        def _(i):
            term = dot_nt(x[...], w[j, tile_at(i), :])
            if first:
                y[s, :, tile_at(i)] = term
            else:
                y[s, :, tile_at(i)] += term

        term = jnp.dot(x[...], b[columns(j), :], preferred_element_type=F32)
        if first:
            r[s] = term
        else:
            r[s] += term

    def arrive(s, k):
        j = mp_at(k)
        remote(
            tok.at[s], xbuf.at[s, j], x_send.at[s, k], x_recv.at[s, j], (dp, j)
        ).wait_recv()
        block(s, j, xbuf.at[s, j], False)

    def gradient(s):
        reduced = r[s].astype(BF16)

        @pl.loop(0, tiles)
        def _(i):
            outputs = y[s, :, tile_at(i)]
            if s == 1:
                outputs = outputs - 0.02 * dot_nt(reduced, dall[0, tile_at(i), :])
            outputs = outputs.astype(BF16).astype(F32)
            e[:, tile_at(i)] = (outputs - tgt[s, :, tile_at(i)].astype(F32)).astype(BF16)
            g[tile_at(i), :] = dot_tn(e[:, tile_at(i)], reduced)

    def scatter_start(s):
        ones = []
        for k in range(1, n_ch + 1):
            c = chip_at(k)
            send1[s, c] = g[owner_rows(c * 2 + 1 - core), :].astype(BF16)
            copy = remote(
                send1.at[s, c], recv1.at[s, c], s1_send.at[s, c], s1_recv.at[s, c], (partner, mp)
            )
            copy.start()
            sends.append(copy)
            ones.append((c, copy))
        for k, (c, copy) in enumerate(ones):
            copy.wait_recv()
            total = g[owner_rows(c * 2 + core), :] + recv1[s, c].astype(F32)
            if k < n_ch - 1:
                send2[s, c] = total.astype(BF16)
                out = remote(
                    send2.at[s, c], recv2.at[s, chip], s2_send.at[s, c], s2_recv.at[s, chip],
                    (c * 2 + core, mp),
                )
                out.start()
                sends.append(out)
            else:
                g[owner_rows(c * 2 + core), :] = total

    def scatter_finish(s):
        total = g[owner_rows(dp), :]
        for k in range(1, n_ch):
            c = chip_at(k)
            remote(
                send2.at[s, c], recv2.at[s, c], s2_send.at[s, c], s2_recv.at[s, c],
                (c * 2 + core, mp),
            ).wait_recv()
            total = total + recv2[s, c].astype(F32)
        projected = total / total_tokens
        first = 0.9 * mom1[...] + 0.1 * projected
        second = 0.95 * mom2[...] + 0.05 * projected * projected
        mom1[...] = first
        mom2[...] = second
        dall[s, owner_rows(dp), :] = (first / (jnp.sqrt(second) + 1e-08)).astype(BF16)

    def direction_copy(s, owner, sem_at, where):
        part = dall.at[s, owner_rows(owner), :]
        return remote(part, part, d_send.at[s, sem_at], d_recv.at[s, owner], where)

    def gather_start(s):
        for k in range(1, n_ch):
            c = chip_at(k)
            copy = direction_copy(s, dp, c, (c * 2 + core, mp))
            copy.start()
            sends.append(copy)
        copy = direction_copy(s, dp, n_ch + chip, (partner, mp))
        copy.start()
        sends.append(copy)

    def gather_forward(s):
        for k in range(1, n_ch):
            c = chip_at(k)
            owner = c * 2 + core
            direction_copy(s, owner, c, (owner, mp)).wait_recv()
            copy = direction_copy(s, owner, n_ch + c, (partner, mp))
            copy.start()
            sends.append(copy)

    def gather_finish(s):
        for k in range(n_ch):
            c = chip_at(k)
            direction_copy(s, c * 2 + 1 - core, n_ch + c, (partner, mp)).wait_recv()

    def lift(j):
        @pl.loop(0, tiles)
        def _(i):
            lifted = dot_nt(dall[0, tile_at(i), :], b[j * fin:(j + 1) * fin, :])
            w[j, tile_at(i), :] = (w[j, tile_at(i), :].astype(F32) - 0.02 * lifted).astype(BF16)

        copy = pltpu.make_async_copy(
            w.at[j], w1_hbm.at[:, j * fin:(j + 1) * fin], o_sem.at[j]
        )
        copy.start()
        return copy

    b_copy.wait()
    w_copies[0].wait()
    block(0, mp, tok.at[0], True)
    block(1, mp, tok.at[1], True)
    for copy in w_copies[1:]:
        copy.wait()
    t_copy.wait()
    m_copy.wait()
    v_copy.wait()
    for k in range(1, n_mp):
        arrive(0, k)
    gradient(0)
    scatter_start(0)
    scatter_finish(0)
    gather_start(0)
    gather_forward(0)
    for k in range(1, n_mp):
        arrive(1, k)
    gather_finish(0)
    gradient(1)
    scatter_start(1)
    outs = [lift(j) for j in range(n_mp)]
    scatter_finish(1)
    gather_start(1)
    m_done = pltpu.make_async_copy(mom1, m_out.at[0], o_sem.at[n_mp])
    v_done = pltpu.make_async_copy(mom2, v_out.at[0], o_sem.at[n_mp + 1])
    m_done.start()
    v_done.start()
    gather_forward(1)
    gather_finish(1)
    d_done = pltpu.make_async_copy(dall.at[1], d1_hbm, o_sem.at[n_mp + 2])
    d_done.start()
    for copy in sends:
        copy.wait_send()
    for copy in outs:
        copy.wait()
    m_done.wait()
    v_done.wait()
    d_done.wait()


def local(n_dp, n_mp, tokens, targets, weight, basis, moment1, moment2):
    steps, toks, fin = tokens.shape
    out_rows, features = weight.shape
    rank = basis.shape[1]
    rows = moment1.shape[1]
    n_ch = n_dp // 2
    hbm = pl.BlockSpec(memory_space=pl.ANY)
    dma = pltpu.SemaphoreType.DMA
    w1, d1, first, second = pl.pallas_call(
        functools.partial(kernel, n_dp, n_mp, toks * n_dp),
        out_shape=(
            jax.ShapeDtypeStruct((out_rows, features), BF16),
            jax.ShapeDtypeStruct((out_rows, rank), BF16),
            jax.ShapeDtypeStruct((1, rows, rank), F32),
            jax.ShapeDtypeStruct((1, rows, rank), F32),
        ),
        in_specs=[pl.BlockSpec(memory_space=pltpu.VMEM)] + [hbm] * 5,
        out_specs=(hbm,) * 4,
        scratch_shapes=[
            pltpu.VMEM((steps, n_mp, toks, fin), BF16),
            pltpu.VMEM((steps, toks, out_rows), BF16),
            pltpu.VMEM((n_mp, out_rows, fin), BF16),
            pltpu.VMEM((features, rank), BF16),
            pltpu.VMEM((rows, rank), F32),
            pltpu.VMEM((rows, rank), F32),
            pltpu.VMEM((steps, toks, out_rows), F32),
            pltpu.VMEM((steps, toks, rank), F32),
            pltpu.VMEM((toks, out_rows), BF16),
            pltpu.VMEM((out_rows, rank), F32),
            pltpu.VMEM((steps, n_ch, rows, rank), BF16),
            pltpu.VMEM((steps, n_ch, rows, rank), BF16),
            pltpu.VMEM((steps, n_ch, rows, rank), BF16),
            pltpu.VMEM((steps, n_ch, rows, rank), BF16),
            pltpu.VMEM((steps, out_rows, rank), BF16),
            dma((n_mp + 4,)),
            dma((steps, n_mp)),
            dma((steps, n_mp)),
            dma((steps, n_ch)),
            dma((steps, n_ch)),
            dma((steps, n_ch)),
            dma((steps, n_ch)),
            dma((steps, n_dp)),
            dma((steps, n_dp)),
            dma((n_mp + 3,)),
        ],
        compiler_params=pltpu.CompilerParams(
            collective_id=0, has_side_effects=True, vmem_limit_bytes=48 * 2**20
        ),
    )(tokens, targets, weight, basis, moment1, moment2)
    lifted = lax.dot_general(
        d1, basis, (((1,), (1,)), ((), ())), preferred_element_type=F32
    )
    return ((w1.astype(F32) - 0.02 * lifted).astype(BF16), first, second)


def solution(mesh):
    in_specs = (
        P(None, "dp", "mp"),
        P(None, "dp", "mp"),
        P("mp", None),
        P(),
        P("mp", "dp", None),
        P("mp", "dp", None),
    )
    out_specs = (P("mp", None), P("mp", "dp", None), P("mp", "dp", None))
    body = functools.partial(local, mesh.shape["dp"], mesh.shape["mp"])
    return jax.shard_map(body, mesh=mesh, in_specs=in_specs, out_specs=out_specs, check_vma=False)
```

time: 294 us -> 104 us (0.35)
  the two profiles are of different devices: /device:TPU:0 before, /device:TPU:9 now
where the time goes in v1:
time: 104 us
  Pallas kernels  88.7 us (85%)
  matrix products  8.97 us (9%)
  local copies, waits for them, and re-layouts  5.38 us (5%)
    pallas_call x1, Pallas kernels, local(): pl.pallas_call(functools.partial(kernel, n_dp, n_mp, toks * n_dp), out_sh...  88.7 us
    dot_general x1, matrix products, local(): lax.dot_general(d1, basis, (((1,), (1,)), ((), ())), preferred_element_ty...  8.97 us
    unnamed x12, local copies, waits for them, and re-layouts  5.38 us

profile of v1, /device:TPU:9, one launch (start us, length us, event | category | flops | bytes accessed | tf_op | source)
XLA Modules:
  0.0 103.7 jit_solution(10702618090697525723)
XLA Ops:
  0.6 0.0 copy-start
  0.6 1.0 copy-done
  1.7 0.0 copy-start.1
  1.7 1.0 %copy-done.1 = bf16[2,128,1024]{2,1,0:T(8,128)(2,1)S(1)} copy-done((bf16[2,128,1024]{2,1,0:T(8,128)(2,1)S(1)}, bf16[2,128,1024]{2,1,0:T(8,128)(2,1)}, u32[]{:S(2)}) %copy-start.1) | copy-done | bytes 524312
  2.7 0.0 copy-start.2
  2.7 0.9 copy-done.2
  3.7 0.0 copy-start.3
  3.7 0.9 copy-done.3
  4.6 0.0 copy-start.4
  4.6 88.7 %shard_map.85 = (bf16[1024,4096]{1,0:T(8,128)(2,1)}, bf16[1024,512]{1,0:T(8,128)(2,1)S(1)}, f32[1,128,512]{2,1,0:T(8,128)S(1)}, f32[1,128,512]{2,1,0:T(8,128)S(1)}) custom-call(bf16[2,128,1024]{2,1,0:T(8,128)(2,1)S(1)} %copy-done, bf16[2,128,1024]{2,1,0:T(8,128)(2,1)S(1)} %copy-done.1, bf16[1024,4096]{1,0:T(8,128)(2,1)} %w_hbm.1, bf16[4096,512]{1,0:T(8,128)(2,1)} %b_hbm.1, ...), custom_call_target="tpu_custom_call" | custom-call | tf_op jit(solution)/shard_map/pallas_call | solution.py:259
  93.3 0.0 copy-done.4
  93.3 9.0 %subtract_convert_fusion = bf16[1024,4096]{1,0:T(8,128)(2,1)} fusion(bf16[1024,4096]{1,0:T(8,128)(2,1)} %get-tuple-element.7, bf16[1024,512]{1,0:T(8,128)(2,1)S(1)} %get-tuple-element.8, bf16[4096,512]{1,0:T(8,128)(2,1)S(1)} %copy-done.4), kind=kOutput, calls=%fused_computation | convolution fusion | flops 4311744512 | bytes 22020096 | tf_op jit(solution)/shard_map/dot_general | solution.py:300
  102.3 0.7 copy.11
  103.0 0.7 copy.12
Async XLA Ops:
  0.6 1.0 %copy-start = (bf16[2,128,1024]{2,1,0:T(8,128)(2,1)S(1)}, bf16[2,128,1024]{2,1,0:T(8,128)(2,1)}, u32[]{:S(2)}) copy-start(bf16[2,128,1024]{2,1,0:T(8,128)(2,1)} %tok.1) | copy-start | bytes 1572868
  1.7 1.0 %copy-start.1 = (bf16[2,128,1024]{2,1,0:T(8,128)(2,1)S(1)}, bf16[2,128,1024]{2,1,0:T(8,128)(2,1)}, u32[]{:S(2)}) copy-start(bf16[2,128,1024]{2,1,0:T(8,128)(2,1)} %tgt_hbm.1) | copy-start | bytes 1572868
  2.7 0.9 copy-start.2
  3.7 0.9 copy-start.3
  4.6 88.7 %copy-start.4 = (bf16[4096,512]{1,0:T(8,128)(2,1)S(1)}, bf16[4096,512]{1,0:T(8,128)(2,1)}, u32[]{:S(2)}) copy-start(bf16[4096,512]{1,0:T(8,128)(2,1)} %b_hbm.1) | copy-start | bytes 12582916

commit v2 on v1

--- a/solution.py
+++ b/solution.py
@@ -68,6 +68,8 @@
     t_copy = pltpu.make_async_copy(tgt_hbm, tgt, l_sem.at[n_mp + 1])
     m_copy = pltpu.make_async_copy(m_hbm.at[0], mom1, l_sem.at[n_mp + 2])
     v_copy = pltpu.make_async_copy(v_hbm.at[0], mom2, l_sem.at[n_mp + 3])
+    k_copy = pltpu.make_async_copy(tok, xbuf.at[:, mp], l_sem.at[n_mp + 4])
+    k_copy.start()
     b_copy.start()
     for copy in w_copies:
         copy.start()
@@ -83,14 +85,53 @@
         pl.semaphore_signal(barrier, inc=1, device_id=peer, device_id_type=pl.DeviceIdType.MESH)
     pl.semaphore_wait(barrier, len(peers))
 
+    def token_copy(s, j, lane, where):
+        part = xbuf.at[s, j]
+        return remote(part, part, x_send.at[s, lane], x_recv.at[s, j], (dp, where))
+
+    def relay(d, down):
+        j = mp + d if down else mp - d
+        there = (j < n_mp) if down else (j >= 0)
+        onward = (mp > 0) if down else (mp < n_mp - 1)
+        to = mp - 1 if down else mp + 1
+        return j, there, onward, token_copy(0, j, 2 * d + int(down), to)
+
+    def relay_step(d, down):
+        j, there, onward, copy = relay(d, down)
+
+        @pl.when(there)
+        def _():
+            if d > 0:
+                copy.wait_recv()
+
+            @pl.when(onward)
+            def _():
+                copy.start()
+
+    def relay_done(d, down):
+        j, there, onward, copy = relay(d, down)
+
+        @pl.when(jnp.logical_and(there, onward))
+        def _():
+            copy.wait_send()
+
+    low = (mp < n_mp // 2).astype(jnp.int32)
+
+    def other_at(i):
+        down = n_mp - 1 - i
+        down = down - (down <= mp).astype(jnp.int32)
+        up = i + (mp <= i).astype(jnp.int32)
+        return low * down + (1 - low) * up
+
     sends = []
-    for s in range(2):
-        for k in range(1, n_mp):
-            copy = remote(
-                tok.at[s], xbuf.at[s, mp], x_send.at[s, k], x_recv.at[s, mp], (dp, mp_at(k))
-            )
-            copy.start()
-            sends.append(copy)
+    k_copy.wait()
+    for d in range(n_mp):
+        for down in (True, False):
+            relay_step(d, down)
+    for i in range(n_mp - 1):
+        copy = token_copy(1, mp, i, other_at(i))
+        copy.start()
+        sends.append(copy)
 
     def block(s, j, x, first):
         @pl.loop(0, tiles)
@@ -107,11 +148,10 @@
         else:
             r[s] += term
 
-    def arrive(s, k):
-        j = mp_at(k)
-        remote(
-            tok.at[s], xbuf.at[s, j], x_send.at[s, k], x_recv.at[s, j], (dp, j)
-        ).wait_recv()
+    def arrive(s, i):
+        j = other_at(i)
+        if s == 1:
+            token_copy(1, j, i, j).wait_recv()
         block(s, j, xbuf.at[s, j], False)
 
     def gradient(s):
@@ -196,10 +236,14 @@
             direction_copy(s, c * 2 + 1 - core, n_ch + c, (partner, mp)).wait_recv()
 
     def lift(j):
-        @pl.loop(0, tiles)
+        width = min(256, fin)
+
+        @pl.loop(0, fin // width)
         def _(i):
-            lifted = dot_nt(dall[0, tile_at(i), :], b[j * fin:(j + 1) * fin, :])
-            w[j, tile_at(i), :] = (w[j, tile_at(i), :].astype(F32) - 0.02 * lifted).astype(BF16)
+            cols = pl.ds(pl.multiple_of(i * width, width), width)
+            from_b = pl.ds(pl.multiple_of(j * fin + i * width, width), width)
+            lifted = dot_nt(dall[0], b[from_b, :])
+            w[j, :, cols] = (w[j, :, cols].astype(F32) - 0.02 * lifted).astype(BF16)
 
         copy = pltpu.make_async_copy(
             w.at[j], w1_hbm.at[:, j * fin:(j + 1) * fin], o_sem.at[j]
@@ -208,23 +252,22 @@
         return copy
 
     b_copy.wait()
-    w_copies[0].wait()
-    block(0, mp, tok.at[0], True)
-    block(1, mp, tok.at[1], True)
-    for copy in w_copies[1:]:
+    for copy in w_copies:
         copy.wait()
+    block(0, mp, xbuf.at[0, mp], True)
     t_copy.wait()
     m_copy.wait()
     v_copy.wait()
-    for k in range(1, n_mp):
-        arrive(0, k)
+    for i in reversed(range(n_mp - 1)):
+        arrive(0, i)
     gradient(0)
     scatter_start(0)
     scatter_finish(0)
     gather_start(0)
+    block(1, mp, xbuf.at[1, mp], True)
     gather_forward(0)
-    for k in range(1, n_mp):
-        arrive(1, k)
+    for i in reversed(range(n_mp - 1)):
+        arrive(1, i)
     gather_finish(0)
     gradient(1)
     scatter_start(1)
@@ -241,11 +284,45 @@
     d_done.start()
     for copy in sends:
         copy.wait_send()
+    for d in range(n_mp):
+        for down in (True, False):
+            relay_done(d, down)
     for copy in outs:
         copy.wait()
     m_done.wait()
     v_done.wait()
     d_done.wait()
+
+
+def last_lift(width, w1, d1, b, first, second, w_out, m_out, v_out, stage, sem, s_sem):
+    m_copy = pltpu.make_async_copy(first, m_out, s_sem.at[0])
+    v_copy = pltpu.make_async_copy(second, v_out, s_sem.at[1])
+    m_copy.start()
+    v_copy.start()
+    features = w1.shape[1]
+    count = features // width
+
+    def put(i, slot):
+        at = pl.ds(pl.multiple_of(i * width, width), width)
+        return pltpu.make_async_copy(stage.at[slot], w_out.at[:, at], sem.at[slot])
+
+    @pl.loop(0, count)
+    def _(i):
+        slot = lax.rem(i, 2)
+
+        @pl.when(i >= 2)
+        def _():
+            put(i - 2, slot).wait()
+
+        at = pl.ds(pl.multiple_of(i * width, width), width)
+        lifted = dot_nt(d1[...], b[at, :])
+        stage[slot] = (w1[:, at].astype(F32) - 0.02 * lifted).astype(BF16)
+        put(i, slot).start()
+
+    for i in range(max(count - 2, 0), count):
+        put(i, i % 2).wait()
+    m_copy.wait()
+    v_copy.wait()
 
 
 def local(n_dp, n_mp, tokens, targets, weight, basis, moment1, moment2):
@@ -254,7 +331,8 @@
     rank = basis.shape[1]
     rows = moment1.shape[1]
     n_ch = n_dp // 2
-    hbm = pl.BlockSpec(memory_space=pl.ANY)
+    hbm = pl.BlockSpec(memory_space=pltpu.HBM)
+    anywhere = pl.BlockSpec(memory_space=pl.ANY)
     dma = pltpu.SemaphoreType.DMA
     w1, d1, first, second = pl.pallas_call(
         functools.partial(kernel, n_dp, n_mp, toks * n_dp),
@@ -264,8 +342,8 @@
             jax.ShapeDtypeStruct((1, rows, rank), F32),
             jax.ShapeDtypeStruct((1, rows, rank), F32),
         ),
-        in_specs=[pl.BlockSpec(memory_space=pltpu.VMEM)] + [hbm] * 5,
-        out_specs=(hbm,) * 4,
+        in_specs=[hbm] * 6,
+        out_specs=(anywhere,) * 4,
         scratch_shapes=[
             pltpu.VMEM((steps, n_mp, toks, fin), BF16),
             pltpu.VMEM((steps, toks, out_rows), BF16),
@@ -282,8 +360,8 @@
             pltpu.VMEM((steps, n_ch, rows, rank), BF16),
             pltpu.VMEM((steps, n_ch, rows, rank), BF16),
             pltpu.VMEM((steps, out_rows, rank), BF16),
-            dma((n_mp + 4,)),
-            dma((steps, n_mp)),
+            dma((n_mp + 5,)),
+            dma((steps, 2 * n_mp)),
             dma((steps, n_mp)),
             dma((steps, n_ch)),
             dma((steps, n_ch)),
@@ -294,13 +372,26 @@
             dma((n_mp + 3,)),
         ],
         compiler_params=pltpu.CompilerParams(
-            collective_id=0, has_side_effects=True, vmem_limit_bytes=48 * 2**20
+            collective_id=0, has_side_effects=True, vmem_limit_bytes=36 * 2**20
         ),
-    )(tokens, targets, weight, basis, moment1, moment2)
-    lifted = lax.dot_general(
-        d1, basis, (((1,), (1,)), ((), ())), preferred_element_type=F32
-    )
-    return ((w1.astype(F32) - 0.02 * lifted).astype(BF16), first, second)
+    )(*[
+        pltpu.with_memory_space_constraint(x, pltpu.HBM)
+        for x in (tokens, targets, weight, basis, moment1, moment2)
+    ])
+    width = min(256, features)
+    vmem = pl.BlockSpec(memory_space=pltpu.VMEM)
+    return pl.pallas_call(
+        functools.partial(last_lift, width),
+        out_shape=(
+            jax.ShapeDtypeStruct((out_rows, features), BF16),
+            jax.ShapeDtypeStruct((1, rows, rank), F32),
+            jax.ShapeDtypeStruct((1, rows, rank), F32),
+        ),
+        in_specs=[vmem] * 5,
+        out_specs=(hbm,) * 3,
+        scratch_shapes=[pltpu.VMEM((2, out_rows, width), BF16), dma((2,)), dma((2,))],
+        compiler_params=pltpu.CompilerParams(vmem_limit_bytes=12 * 2**20),
+    )(w1, d1, basis, first, second)
 
 
 def solution(mesh):

time: 104 us -> 94.8 us (0.912)
  the two profiles are of different devices: /device:TPU:9 before, /device:TPU:0 now
where the time goes in v2:
time: 94.8 us; the launch traced here: 94.6 us
  Pallas kernels  93.9 us (99%)
    pallas_call x1, Pallas kernels, local(): pl.pallas_call(functools.partial(kernel, n_dp, n_mp, toks * n_dp), out_sh...  83.3 us
    pallas_call x1, Pallas kernels, local(): pl.pallas_call(functools.partial(last_lift, width), out_shape=(jax.ShapeD...  10.6 us

profile of v2, /device:TPU:0, one launch (start us, length us, event | category | flops | bytes accessed | tf_op | source)
XLA Modules:
  0.0 94.6 jit_solution(9805962882211346373)
XLA Ops:
  0.6 0.0 copy-start
  0.6 83.3 %shard_map.85 = (bf16[1024,4096]{1,0:T(8,128)(2,1)S(1)}, bf16[1024,512]{1,0:T(8,128)(2,1)S(1)}, f32[1,128,512]{2,1,0:T(8,128)S(1)}, f32[1,128,512]{2,1,0:T(8,128)S(1)}) custom-call(bf16[2,128,1024]{2,1,0:T(8,128)(2,1)} %tok.1, bf16[2,128,1024]{2,1,0:T(8,128)(2,1)} %tgt_hbm.1, bf16[1024,4096]{1,0:T(8,128)(2,1)} %w_hbm.1, bf16[4096,512]{1,0:T(8,128)(2,1)} %b.1, ...), custom_call_target="tpu_custom_call" | custom-call | tf_op jit(solution)/shard_map/pallas_call | solution.py:337
  84.0 0.0 copy-done
  84.0 10.6 %shard_map.86 = (bf16[1024,4096]{1,0:T(8,128)(2,1)}, f32[1,128,512]{2,1,0:T(8,128)}, f32[1,128,512]{2,1,0:T(8,128)}) custom-call(bf16[1024,4096]{1,0:T(8,128)(2,1)S(1)} %get-tuple-element.7.w1, bf16[1024,512]{1,0:T(8,128)(2,1)S(1)} %get-tuple-element.8.d1, bf16[4096,512]{1,0:T(8,128)(2,1)S(1)} %copy-done, f32[1,128,512]{2,1,0:T(8,128)S(1)} %get-tuple-element.9.first, ...), custom_call_target="tpu_custom_call" | custom-call | tf_op jit(solution)/shard_map/pallas_call | solution.py:383
Async XLA Ops:
  0.6 83.4 %copy-start = (bf16[4096,512]{1,0:T(8,128)(2,1)S(1)}, bf16[4096,512]{1,0:T(8,128)(2,1)}, u32[]{:S(2)}) copy-start(bf16[4096,512]{1,0:T(8,128)(2,1)} %b.1) | copy-start | bytes 12582916
